TPU v7x, 256 devices: a whole 4x4x8 slice. The times are simulated.
256 devices in a mesh: section: 2 (over x_hi), lat: 4 (over x_lo, core), lon: 32 (over y, z).
Axes of the slice: x: 4 (x_hi: 2, x_lo: 2; x = x_hi * 2 + x_lo), y: 4, z: 8, core: 2. Of those that a mesh axis runs over, the one named last changes fastest.
Arguments:
- window_input: bfloat16 [2, 16, 2176, 256], P(None, 'lat', 'lon'), may hold values from -8 to 8
- output_cotangent: bfloat16 [2, 16, 2176, 256], P(None, 'lat', 'lon'), may hold values from -6 to 6
- ocean_mask: int32 [16, 2176], P('lat', 'lon'), may hold values 0 or 1
- dw_kernel: bfloat16 [2, 49, 256], P('section'), may hold values from -1.5 to 1.5
- channel_params: bfloat16 [2, 5, 256], P('section'), may hold values from -1.5 to 1.5
- up_weight: bfloat16 [2, 256, 1024], P('section'), may hold values from -0.375 to 0.375
- up_bias: bfloat16 [2, 1024], P('section'), may hold values from -3 to 3
- down_weight: bfloat16 [2, 1024, 256], P('section'), may hold values from -0.1875 to 0.1875
Outputs:
- boundary: bfloat16 [2, 2, 16, 2176, 256], P('section', None, 'lat', 'lon')
- grad_kernel: float32 [2, 49, 256], P('section')
- grad_channels: float32 [2, 5, 256], P('section')
- grad_up: float32 [2, 256, 1024], P('section')
- grad_up_bias: float32 [2, 1024], P('section')
- grad_down: float32 [2, 1024, 256], P('section')
All inputs are finite; a program needn't handle non-finite values. No bound on the sum of `ocean_mask` on one device may be relied on, other than what follows from the above.
Results may differ from a plain program's by a relative error of at most 0.012.
Values may be sent and summed in bfloat16 or wider, within the bound.
A program may use at most 128 MiB of HBM per device.

v0:
```python
import math
import jax
import jax.numpy as jnp
from jax import lax
from jax.sharding import PartitionSpec as P

KERNEL = 7
ROWS_DEV = 4
COLS_DEV = 68
BATCH = 2
norm_eps = 1e-06
gelu_scale = 0.7978845608028654
gelu_cubic = 0.044715
rows_contract = (((0,), (0,)), ((), ()))
cols_contract = (((1,), (1,)), ((), ()))


def padded_2(block, sides, width, periodic):
    for axis, dim in sides:
        count = lax.axis_size(axis)
        forward = [(i, i + 1) for i in range(count - 1)]
        if periodic:
            forward.append((count - 1, 0))
        backward = [(target, source) for source, target in forward]
        low = lax.ppermute(
            lax.slice_in_dim(block, block.shape[dim] - width, None, axis=dim), axis, forward
        )
        high = lax.ppermute(lax.slice_in_dim(block, 0, width, axis=dim), axis, backward)
        block = jnp.concatenate([low, block, high], axis=dim)
    return block


def from_behind(value, axis, by):
    count = lax.axis_size(axis)
    pairs = [(i, i + by) for i in range(count) if 0 <= i + by < count]
    return lax.ppermute(value, axis, pairs)


def gelu_value(values):
    inner = gelu_scale * (values + gelu_cubic * values * values * values)
    return 0.5 * values * (1.0 + jnp.tanh(inner))


def gelu_slope(values):
    tangent = jnp.tanh(gelu_scale * (values + gelu_cubic * values * values * values))
    return 0.5 * (1.0 + tangent) + 0.5 * values * (1.0 - tangent * tangent) * gelu_scale * (
        1.0 + 3.0 * gelu_cubic * values * values
    )


def depthwise(padded, kernel, row_count, col_count):
    summed = jnp.zeros((padded.shape[0], row_count, col_count, padded.shape[3]), jnp.float32)
    for offset in range(KERNEL * KERNEL):
        row_off, col_off = divmod(offset, KERNEL)
        window = padded[:, row_off : row_off + row_count, col_off : col_off + col_count, :]
        summed = summed + window.astype(jnp.float32) * kernel[offset].astype(jnp.float32)
    return summed


def kernel_grads(padded, grad_conv, row_count, col_count):
    channels = grad_conv.shape[-1]
    grad_wide = grad_conv.astype(jnp.float32)
    tap_sums = []
    for offset in range(KERNEL * KERNEL):
        row_off, col_off = divmod(offset, KERNEL)
        window = padded[:, row_off : row_off + row_count, col_off : col_off + col_count, :].astype(
            jnp.float32
        )
        tap_sums.append(jnp.sum((grad_wide * window).reshape(-1, channels), axis=0))
    return (jnp.stack(tap_sums), jnp.sum(grad_wide.reshape(-1, channels), axis=0))


def cell_forward(conv_out, inputs, sea_mask, params, w_up, b_up, w_down):
    average = jnp.mean(conv_out, axis=-1, keepdims=True)
    centered = conv_out - average
    inverse = lax.rsqrt(jnp.mean(centered * centered, axis=-1, keepdims=True) + norm_eps)
    normed = centered * inverse
    scaled = (normed * params[1].astype(jnp.float32) + params[2].astype(jnp.float32)).astype(
        jnp.bfloat16
    )
    channels = scaled.shape[-1]
    flat_rows = scaled.reshape(-1, channels)
    hidden = jnp.dot(flat_rows, w_up, preferred_element_type=jnp.float32) + b_up.astype(jnp.float32)
    active = gelu_value(hidden).astype(jnp.bfloat16)
    branch = jnp.dot(active, w_down, preferred_element_type=jnp.float32) + params[3].astype(
        jnp.float32
    )
    branch = branch.reshape(conv_out.shape)
    output = (
        sea_mask * (inputs.astype(jnp.float32) + params[4].astype(jnp.float32) * branch)
    ).astype(jnp.bfloat16)
    return (output, (normed, inverse, flat_rows, hidden, active, branch))


def cell_backward(saved, sea_mask, cotangent, params, w_up, w_down):
    normed, inverse, flat_rows, hidden, active, branch = saved
    channels = normed.shape[-1]
    upstream = sea_mask * cotangent.astype(jnp.float32)
    grad_scale = jnp.sum((upstream * branch).reshape(-1, channels), axis=0)
    grad_branch = (
        (params[4].astype(jnp.float32) * upstream).astype(jnp.bfloat16).reshape(-1, channels)
    )
    grad_down = lax.dot_general(
        active, grad_branch, rows_contract, preferred_element_type=jnp.float32
    )
    grad_out_bias = jnp.sum(grad_branch.astype(jnp.float32), axis=0)
    grad_active = lax.dot_general(
        grad_branch, w_down, cols_contract, preferred_element_type=jnp.float32
    )
    grad_hidden = (grad_active * gelu_slope(hidden)).astype(jnp.bfloat16)
    grad_up = lax.dot_general(
        flat_rows, grad_hidden, rows_contract, preferred_element_type=jnp.float32
    )
    grad_up_bias = jnp.sum(grad_hidden.astype(jnp.float32), axis=0)
    grad_scaled = lax.dot_general(
        grad_hidden, w_up, cols_contract, preferred_element_type=jnp.float32
    )
    grad_scaled = grad_scaled.reshape(normed.shape)
    grad_gain = jnp.sum((grad_scaled * normed).reshape(-1, channels), axis=0)
    grad_shift = jnp.sum(grad_scaled.reshape(-1, channels), axis=0)
    grad_normed = grad_scaled * params[1].astype(jnp.float32)
    first_mean = jnp.mean(grad_normed, axis=-1, keepdims=True)
    second_mean = jnp.mean(grad_normed * normed, axis=-1, keepdims=True)
    grad_conv = (inverse * (grad_normed - first_mean - normed * second_mean)).astype(jnp.bfloat16)
    small = (grad_gain, grad_shift, grad_out_bias, grad_scale)
    return (grad_conv, upstream, small, grad_up, grad_up_bias, grad_down)


def halo_field(field):
    reach = KERNEL // 2
    beside_all = padded_2(field, (("lon", 2),), reach, True)
    return padded_2(beside_all, (("lat", 1),), reach, False)


def run_forward(field, sea_mask, weights):
    kernel, params, w_up, b_up, w_down = weights
    padded = halo_field(field)
    conv_out = depthwise(padded, kernel, field.shape[1], field.shape[2]) + params[0].astype(
        jnp.float32
    )
    output, saved = cell_forward(conv_out, field, sea_mask, params, w_up, b_up, w_down)
    return (output, (padded, saved))


def run_backward(stored, sea_mask, weights, cotangent):
    kernel, params, w_up, b_up, w_down = weights
    padded, saved = stored
    row_count, col_count = (cotangent.shape[1], cotangent.shape[2])
    grad_conv, upstream, small, grad_up, grad_bias, grad_down = cell_backward(
        saved, sea_mask, cotangent, params, w_up, w_down
    )
    tap_sums, bias_sum = kernel_grads(padded, grad_conv, row_count, col_count)
    spread = depthwise(halo_field(grad_conv), kernel[::-1], row_count, col_count)
    grad_input = (upstream + spread).astype(jnp.bfloat16)
    return (grad_input, (tap_sums, jnp.stack((bias_sum,) + small), grad_up, grad_bias, grad_down))


def on_device(
    window_input,
    output_cotangent,
    ocean_mask,
    dw_kernel,
    channel_params,
    up_weight,
    up_bias,
    down_weight,
):
    section = lax.axis_index("section")
    first_section = section == 0
    sea_mask = ocean_mask.astype(jnp.float32)[None, :, :, None]
    batch_size = window_input.shape[0]
    local = (dw_kernel[0], channel_params[0], up_weight[0], up_bias[0], down_weight[0])
    micro = 1
    size_micro = batch_size // micro
    zero_field = jnp.zeros((size_micro,) + window_input.shape[1:], jnp.bfloat16)
    received = zero_field
    stored = []
    outputs = []
    for tick in range(micro + 1):
        if tick < micro:
            own_part = window_input
        else:
            own_part = zero_field
        current = jnp.where(first_section, own_part, received)
        result, kept = run_forward(current, sea_mask, local)
        stored.append(kept)
        outputs.append(result)
        if tick < micro:
            received = from_behind(result, "section", 1)
    received = zero_field
    grad_inputs = []
    totals = None
    for tick in range(micro + 1):
        if tick < micro:
            own_part = output_cotangent
        else:
            own_part = zero_field
        current = jnp.where(first_section, received, own_part)
        kept = jax.tree.map(
            lambda before, behind: jnp.where(first_section, before, behind),
            stored[max(tick - 1, 0)],
            stored[min(tick + 1, micro)],
        )
        grad_input, grads = run_backward(kept, sea_mask, local, current)
        counted = jnp.where(
            first_section, 1.0 if tick >= 1 else 0.0, 1.0 if tick < micro else 0.0
        ).astype(jnp.float32)
        weighted = jax.tree.map(lambda member: member * counted, grads)
        if totals is None:
            totals = weighted
        else:
            totals = jax.tree.map(jnp.add, totals, weighted)
        grad_inputs.append(grad_input)
        if tick < micro:
            received = from_behind(grad_input, "section", -1)
    final = jnp.concatenate(outputs[1:], axis=0)
    starts = jnp.concatenate(grad_inputs[1:], axis=0)
    boundary = jnp.where(first_section, starts, final)[None]
    owned = tuple((member[None] for member in totals))
    summed = lax.psum((owned[0], owned[1], owned[2], owned[3], owned[4]), ("lat", "lon"))
    factor = 1.0 / math.sqrt(BATCH * ROWS_DEV * COLS_DEV)
    return (
        boundary,
        summed[0] * factor,
        summed[1] * factor,
        summed[2] * factor,
        summed[3] * factor,
        summed[4] * factor,
    )


def solution(mesh):
    in_specs = (
        P(None, "lat", "lon", None),
        P(None, "lat", "lon", None),
        P("lat", "lon"),
        P("section", None, None),
        P("section", None, None),
        P("section", None, None),
        P("section", None),
        P("section", None, None),
    )
    out_specs = (
        P("section", None, "lat", "lon", None),
        P("section", None, None),
        P("section", None, None),
        P("section", None, None),
        P("section", None),
        P("section", None, None),
    )
    return jax.shard_map(
        on_device, mesh=mesh, in_specs=in_specs, out_specs=out_specs, check_vma=False
    )
```

profile of v0, /device:TPU:4, one launch (start us, length us, event | category | flops | bytes accessed | tf_op | source)
XLA Modules:
  0.0 1807.4 jit_solution(11287534964740938511)
XLA Ops:
  8.4 8.4 collective-permute-start.1
  18.9 4.9 collective-permute-done
  24.0 1.3 collective-permute-start.2
  25.3 1.3 collective-permute-start.3
  28.0 2.1 collective-permute-done.3
  30.9 5.6 fusion.257
  38.1 3.1 fusion.4
  42.2 2.0 convolution_add_fusion.1
  45.4 1.6 multiply_convert_fusion.5
  47.0 1.3 collective-permute-start.4
  48.2 8.8 collective-permute-done.4
  57.6 1.6 collective-permute-start.5
  59.2 1.7 collective-permute-done.6
  60.9 3.7 collective-permute-done.5
  65.6 3.9 collective-permute-start.7
  69.6 1.5 collective-permute-start.8
  71.1 1.7 reshape.2386
  73.1 2.0 collective-permute-done.8
  76.1 5.6 fusion.255
  83.1 4.7 fusion.9
  87.9 1.3 convert_reduce_fusion.3
  91.4 2.2 multiply_reduce_fusion.3
  93.7 1.8 maximum_select_fusion
  95.5 1.7 fusion.145
  98.3 1.8 fusion.146
  100.1 2.0 collective-permute-start.9
  103.8 3.3 collective-permute-done.9
  107.3 5.4 collective-permute-start.11
  112.7 1.5 collective-permute-start.12
  114.2 1.9 convolution_add_fusion
  117.4 4.7 add_convert_fusion.1
  122.2 1.3 collective-permute-start.13
  123.5 1.9 reshape.2391
  127.7 2.0 multiply_reduce_fusion.2
  129.8 2.8 convert_reduce_fusion.2
  132.6 1.9 fusion.254
  135.9 1.7 fusion.219
  138.7 1.9 fusion.220
  143.4 1.7 collective-permute-start.14
  145.1 1.6 fusion.16
  146.8 1.7 fusion.18
  149.3 553.0 %all-reduce = (f32[1,49,256]{2,0,1:T(1,128)S(1)}, f32[1,5,256]{2,0,1:T(1,128)S(1)}, f32[1,1024]{1,0:T(1,128)S(1)}) all-reduce(f32[1,49,256]{2,0,1:T(1,128)S(1)} %multiply_add_fusion.3, f32[1,5,256]{2,0,1:T(1,128)S(1)} %multiply_add_fusion.4, f32[1,1024]{1,0:T(1,128)S(1)} %bitcast.416), channel_id=1, replica_groups=mesh['section'=2,'lat'=4,'lon'=32] {'lat','lon'}, use_global_device_ids=true, to_apply=%region_106.107 | all-reduce | flops 14848 | bytes 118784 | tf_op jit(solution)/shard_map/psum | solution.py:220
  703.4 1.4 collective-permute-start.16
  704.8 1.3 collective-permute-start.17
  707.4 4.9 collective-permute-done.17
  712.8 5.5 fusion.252
  719.1 1078.0 %all-reduce.4.cloned.1.call-done = (f32[1,256,1024]{2,1,0:T(8,128)}, f32[1,1024,256]{2,1,0:T(8,128)}) async-done(((f32[1,256,1024]{2,1,0:T(8,128)}, f32[1,1024,256]{2,1,0:T(8,128)}), (f32[1,256,1024]{2,1,0:T(8,128)}, f32[1,1024,256]{2,1,0:T(8,128)})) %all-reduce.4.cloned.1.call-update) | async-done | bytes 2097168 | tf_op jit(solution)/shard_map/psum | solution.py:220
  1797.0 2.4 broadcast_multiply_fusion.1
  (554 shorter events, 30.5 us)
Async XLA Ops:
  7.2 31.0 %copy-start = (bf16[1,256,1024]{2,1,0:T(8,128)(2,1)S(1)}, bf16[1,256,1024]{2,1,0:T(8,128)(2,1)}, u32[]{:S(2)}) copy-start(bf16[1,256,1024]{2,1,0:T(8,128)(2,1)} %param.13) | copy-start | bytes 1572868
  7.2 1789.8 %all-reduce.4.cloned.1.call-start = ((), (), s32[]{:S(2)}) async-start(), calls=%async_computation | async-start | bytes 4194304 | tf_op jit(solution)/shard_map/psum | solution.py:220
  7.2 19.3 %copy-start.173 = (bf16[1,5,256]{2,1,0:T(8,128)(2,1)S(1)}, bf16[1,5,256]{2,1,0:T(8,128)(2,1)}, u32[]{:S(2)}) copy-start(bf16[1,5,256]{2,1,0:T(8,128)(2,1)} %param.12) | copy-start | bytes 7684
  7.2 19.9 %copy-start.182 = (bf16[1,1024]{1,0:T(2,128)(2,1)S(1)}, bf16[1,1024]{1,0:T(2,128)(2,1)}, u32[]{:S(2)}) copy-start(bf16[1,1024]{1,0:T(2,128)(2,1)} %param.14) | copy-start | bytes 6148
  7.3 20.5 %copy-start.184 = (s32[4,68]{1,0:T(4,128)S(1)}, s32[4,68]{1,0:T(4,128)}, u32[]{:S(2)}) copy-start(s32[4,68]{1,0:T(4,128)} %param.10) | copy-start | bytes 3268
  7.3 20.5 %copy-start.32 = (bf16[1,49,256]{2,1,0:T(8,128)(2,1)S(1)}, bf16[1,49,256]{2,1,0:T(8,128)(2,1)}, u32[]{:S(2)}) copy-start(bf16[1,49,256]{2,1,0:T(8,128)(2,1)} %param.11) | copy-start | bytes 75268
  8.4 10.5 collective-permute-start.1
  16.8 7.1 collective-permute-start
  17.8 13.1 copy-start.39
  17.8 13.1 copy-start.42
  17.8 13.0 copy-start.45
  17.8 13.0 copy-start.48
  17.8 58.0 %copy-start.33 = (f32[1,1,256]{2,1,0:T(1,128)}, f32[1,1,256]{2,1,0:T(1,128)S(1)}, u32[]{:S(2)}) copy-start(f32[1,1,256]{2,1,0:T(1,128)S(1)} %get-tuple-element.177) | copy-start | bytes 3076
  17.8 58.0 %copy-start.35 = (f32[1,1,256]{2,1,0:T(1,128)}, f32[1,1,256]{2,1,0:T(1,128)S(1)}, u32[]{:S(2)}) copy-start(f32[1,1,256]{2,1,0:T(1,128)S(1)} %get-tuple-element.178) | copy-start | bytes 3076
  17.8 58.0 %copy-start.37 = (f32[1,1,256]{2,1,0:T(1,128)}, f32[1,1,256]{2,1,0:T(1,128)S(1)}, u32[]{:S(2)}) copy-start(f32[1,1,256]{2,1,0:T(1,128)S(1)} %get-tuple-element.179) | copy-start | bytes 3076
  18.8 12.1 copy-start.51
  18.8 12.1 copy-start.54
  18.8 12.1 copy-start.58
  18.8 12.1 copy-start.62
  18.8 12.1 copy-start.66
  18.8 12.1 copy-start.70
  18.8 12.1 copy-start.74
  18.8 12.1 copy-start.78
  18.8 12.1 copy-start.82
  18.9 12.1 copy-start.86
  18.9 12.1 copy-start.90
  24.0 4.0 collective-permute-start.2
  25.3 4.8 collective-permute-start.3
  45.3 36.4 %copy-start.4 = (f32[2,4,68,256]{3,2,1,0:T(8,128)}, f32[2,4,68,256]{3,2,1,0:T(8,128)S(1)}, u32[]{:S(2)}) copy-start(f32[2,4,68,256]{3,2,1,0:T(8,128)S(1)} %reshape.2385) | copy-start | bytes 1671172
  47.0 10.1 collective-permute-start.4
  57.1 3.8 collective-permute-start.6
  57.6 7.1 collective-permute-start.5
  65.6 7.5 collective-permute-start.7
  69.6 5.5 collective-permute-start.8
  100.1 14.1 copy-start.25
  100.1 3.7 collective-permute-start.10
  100.1 7.1 collective-permute-start.9
  107.3 9.2 collective-permute-start.11
  112.7 4.0 collective-permute-start.12
  122.2 5.5 collective-permute-start.13
  143.0 559.9 %collective-permute-start.15 = (bf16[2,4,3,256]{3,2,1,0:T(4,128)(2,1)S(1)}, bf16[2,4,3,256]{3,2,1,0:T(4,128)(2,1)S(1)}, u32[]{:S(2)}, u32[]{:S(2)}) collective-permute-start(bf16[2,4,3,256]{3,2,1,0:T(4,128)(2,1)S(1)} %get-tuple-element.158), channel_id=1, source_target_pairs={{1,0},{2,1},{3,2},{4,3},{5,4},{6,5},{7,6},{8,7},{9,8},{10,9},{11,1... | collective-permute-start | bytes 36872 | tf_op jit(solution)/shard_map/ppermute | solution.py:28
  143.4 559.5 %collective-permute-start.14 = (bf16[2,4,3,256]{3,2,1,0:T(4,128)(2,1)S(1)}, bf16[2,4,3,256]{3,2,1,0:T(4,128)(2,1)S(1)}, u32[]{:S(2)}, u32[]{:S(2)}) collective-permute-start(bf16[2,4,3,256]{3,2,1,0:T(4,128)(2,1)S(1)} %get-tuple-element.157), channel_id=1, source_target_pairs={{0,1},{1,2},{2,3},{3,4},{4,5},{5,6},{6,7},{7,8},{8,9},{9,10},{10,1... | collective-permute-start | bytes 36872 | tf_op jit(solution)/shard_map/ppermute | solution.py:25
  703.1 9.4 copy-start.5
  703.1 9.4 copy-start.17
  703.1 9.4 copy-start.57
  703.1 9.4 copy-start.61
  703.4 4.0 collective-permute-start.16
  704.8 7.5 collective-permute-start.17
  (158 other events, 654.4 us)
Sparse Core Ops, SparseCore 0:
  703.0 1093.9 all-reduce.3
where the time goes:
time: 1810 us
  waiting for transfers between devices  1110 us (61%)
  blocking collectives  553 us (31%)
  other arithmetic  51.6 us (3%)
  starting transfers between devices  34.9 us (2%)
  matrix products  23.5 us (1%)
    psum x1, waiting for transfers between devices, on_device(): lax.psum((owned[0], owned[1], owned[2], owned[3], owned[4]), ('lat', 'lon'))  1080 us
    psum x1, blocking collectives, on_device(): lax.psum((owned[0], owned[1], owned[2], owned[3], owned[4]), ('lat', 'lon'))  553 us
  transfers between devices with their start and end apart: 19, of which 12 were waited for; matrix products, arithmetic and copies ran while one was open for 1% of the time, Pallas kernels for 0%

commit v1 on v0

--- a/solution.py
+++ b/solution.py
@@ -217,7 +217,7 @@
     starts = jnp.concatenate(grad_inputs[1:], axis=0)
     boundary = jnp.where(first_section, starts, final)[None]
     owned = tuple((member[None] for member in totals))
-    summed = lax.psum((owned[0], owned[1], owned[2], owned[3], owned[4]), ("lat", "lon"))
+    summed = lax.psum(lax.psum((owned[0], owned[1], owned[2], owned[3], owned[4]), "lat"), "lon")
     factor = 1.0 / math.sqrt(BATCH * ROWS_DEV * COLS_DEV)
     return (
         boundary,

time: 1810 us -> 459 us (0.25)
  waiting for transfers between devices: 1110 us -> 169 us
  blocking collectives: 553 us -> 156 us
    psum x1 -> x2, waiting for transfers between devices: 1080 us -> 137 us  [the longest x1 137 us: on_device(): lax.psum(lax.psum((owned[0], owned[1], owned[2], owned[3], owned[4]), 'la...]
    psum x1 -> x2, blocking collectives: 553 us -> 156 us  [the longest x1 142 us: on_device(): lax.psum(lax.psum((owned[0], owned[1], owned[2], owned[3], owned[4]), 'la...]
  transfers between devices with their start and end apart: 19 -> 20, of which waited for: 12 -> 12; matrix products, arithmetic and copies ran while one was open for 1% -> 5% of each run, Pallas kernels for 0% -> 0%
where the time goes in v1:
time: 459 us; the launch traced here: 458 us
  waiting for transfers between devices  169 us (37%)
  blocking collectives  156 us (34%)
  other arithmetic  47.8 us (10%)
  starting transfers between devices  35.8 us (8%)
  matrix products  19.6 us (4%)
  between operations  16.5 us (4%)
  local copies, waits for them, and re-layouts  13.8 us (3%)
    psum x1, blocking collectives, on_device(): lax.psum(lax.psum((owned[0], owned[1], owned[2], owned[3], owned[4]), 'la...  142 us
    psum x1, waiting for transfers between devices, on_device(): lax.psum(lax.psum((owned[0], owned[1], owned[2], owned[3], owned[4]), 'la...  137 us
    ppermute x8, starting transfers between devices, padded_2(): lax.ppermute(lax.slice_in_dim(block, block.shape[dim] - width, None, axis...  17.9 us
    ppermute x8, starting transfers between devices, padded_2(): lax.ppermute(lax.slice_in_dim(block, 0, width, axis=dim), axis, backward)  14.4 us
    psum x1, blocking collectives, on_device(): lax.psum((owned[0], owned[1], owned[2], owned[3], owned[4]), 'lat')  14.1 us
    ppermute x8, waiting for transfers between devices, padded_2(): lax.ppermute(lax.slice_in_dim(block, block.shape[dim] - width, None, axis...  12 us
    ppermute x8, waiting for transfers between devices, padded_2(): lax.ppermute(lax.slice_in_dim(block, 0, width, axis=dim), axis, backward)  10.5 us
    reduce_sum x2, other arithmetic, cell_forward(): average = jnp.mean(conv_out, axis=-1, keepdims=True)  9.75 us
  transfers between devices with their start and end apart: 20, of which 12 were waited for; matrix products, arithmetic and copies ran while one was open for 5% of the time, Pallas kernels for 0%

profile of v1, /device:TPU:4, one launch (start us, length us, event | category | flops | bytes accessed | tf_op | source)
XLA Modules:
  0.0 458.2 jit_solution(3897846480459124218)
XLA Ops:
  8.4 8.4 %collective-permute-start.1 = (bf16[2,4,3,256]{3,2,1,0:T(4,128)(2,1)S(1)}, bf16[2,4,3,256]{3,2,1,0:T(4,128)(2,1)S(1)}, u32[]{:S(2)}, u32[]{:S(2)}) collective-permute-start(bf16[2,4,3,256]{3,2,1,0:T(4,128)(2,1)S(1)} %get-tuple-element.169), channel_id=1, source_target_pairs={{1,0},{2,1},{3,2},{4,3},{5,4},{6,5},{7,6},{8,7},{9,8},{10,9},{11,1... | collective-permute-start | bytes 36872 | tf_op jit(solution)/shard_map/ppermute | solution.py:28
  18.7 5.1 %collective-permute-done = bf16[2,4,3,256]{3,2,1,0:T(4,128)(2,1)S(1)} collective-permute-done((bf16[2,4,3,256]{3,2,1,0:T(4,128)(2,1)S(1)}, bf16[2,4,3,256]{3,2,1,0:T(4,128)(2,1)S(1)}, u32[]{:S(2)}, u32[]{:S(2)}) %collective-permute-start) | collective-permute-done | bytes 12320 | tf_op jit(solution)/shard_map/ppermute | solution.py:25
  24.0 1.3 collective-permute-start.2
  25.3 1.3 collective-permute-start.3
  28.0 2.1 collective-permute-done.3
  30.8 4.8 %fusion.257 = (f32[2,4,68]{2,1,0:T(4,128)S(1)}, f32[2,4,68,256]{3,2,1,0:T(8,128)S(1)}) fusion(f32[256]{0:T(256)S(1)} %bitcast.424, f32[256]{0:T(256)S(1)} %bitcast.332, bf16[2,7,74,256]{3,2,1,0:T(8,128)(2,1)S(1)} %get-tuple-element.157, f32[256]{0:T(256)S(1)} %bitcast.336, f32[256]{0:T(256)S(1)} %bitcast.224, f32[256]{0:T(256)S(1)} %bitcast.228, ...), kind=kLoop, calls=%fused_computation.622 | loop fusion | flops 23117280 | bytes 12611712 | tf_op jit(solution)/shard_map/reduce_sum | solution.py:74
  36.5 2.3 fusion.4
  41.1 1.3 collective-permute-start.4
  42.4 8.8 %collective-permute-done.4 = bf16[2,4,68,256]{3,2,1,0:T(8,128)(2,1)S(1)} collective-permute-done((bf16[2,4,68,256]{3,2,1,0:T(8,128)(2,1)S(1)}, bf16[2,4,68,256]{3,2,1,0:T(8,128)(2,1)S(1)}, u32[]{:S(2)}, u32[]{:S(2)}) %collective-permute-start.4) | collective-permute-done | bytes 278560 | tf_op jit(solution)/shard_map/ppermute | solution.py:36
  51.6 1.8 collective-permute-start.5
  53.4 1.7 collective-permute-done.6
  55.1 3.6 collective-permute-done.5
  59.5 4.0 collective-permute-start.7
  63.5 1.5 collective-permute-start.8
  66.0 2.8 collective-permute-done.8
  69.7 4.9 %fusion.255 = (f32[2,4,68]{2,1,0:T(4,128)S(1)}, f32[2,4,68,256]{3,2,1,0:T(8,128)S(1)}) fusion(f32[256]{0:T(256)S(1)} %bitcast.425, f32[256]{0:T(256)S(1)} %bitcast.333, bf16[2,7,74,256]{3,2,1,0:T(8,128)(2,1)S(1)} %get-tuple-element.153, f32[256]{0:T(256)S(1)} %bitcast.337, f32[256]{0:T(256)S(1)} %bitcast.225, f32[256]{0:T(256)S(1)} %bitcast.229, ...), kind=kLoop, calls=%fused_computation.621 | loop fusion | flops 23117280 | bytes 12611712 | tf_op jit(solution)/shard_map/reduce_sum | solution.py:74
  75.3 4.7 %fusion.9 = (f32[544,1024]{1,0:T(8,128)S(1)}, bf16[544,1024]{1,0:T(8,128)(2,1)}) fusion(f32[544,1024]{1,0:T(8,128)} %get-tuple-element.229, f32[1024]{0:T(1024)S(1)} %bitcast.533, pred[]{:T(512)S(6)} %eq.3, bf16[544,256]{1,0:T(8,128)(2,1)S(1)} %reshape.2387, bf16[1,256,1024]{2,1,0:T(8,128)(2,1)S(1)} %copy-done), kind=kOutput, calls=%fused_computation.115 | convolution fusion | flops 301367296 | bytes 6377473 | tf_op jit(solution)/shard_map/dot_general | solution.py:83
  80.1 1.3 convert_reduce_fusion.3
  81.4 1.1 fusion.253
  83.4 2.2 multiply_reduce_fusion.3
  85.8 1.9 maximum_select_fusion
  87.6 1.7 fusion.145
  90.4 1.9 fusion.146
  92.3 2.0 collective-permute-start.9
  96.0 3.3 collective-permute-done.9
  99.5 5.4 %collective-permute-start.11 = (bf16[2,3,74,256]{3,2,1,0:T(8,128)(2,1)S(1)}, bf16[2,3,74,256]{3,2,1,0:T(8,128)(2,1)S(1)}, u32[]{:S(2)}, u32[]{:S(2)}) collective-permute-start(bf16[2,3,74,256]{3,2,1,0:T(8,128)(2,1)S(1)} %get-tuple-element.150), channel_id=1, source_target_pairs={{0,32},{32,64},{64,96},{1,33},{33,65},{65,97},{2,34},{34,66},{66,9... | collective-permute-start | bytes 681992 | tf_op jit(solution)/shard_map/ppermute | solution.py:25
  104.9 1.5 collective-permute-start.12
  106.4 1.3 convolution_add_fusion
  109.1 5.4 %add_convert_fusion.1 = bf16[2,4,68,256]{3,2,1,0:T(8,128)(2,1)} fusion(bf16[2,4,68,256]{3,2,1,0:T(8,128)(2,1)S(1)} %get-tuple-element.135, bf16[2,4,3,256]{3,2,1,0:T(4,128)(2,1)S(1)} %collective-permute-done.10, bf16[2,4,3,256]{3,2,1,0:T(4,128)(2,1)S(1)} %collective-permute-done.9, bf16[2,7,74,256]{3,2,1,0:T(8,128)(2,1)S(1)} %get-tuple-element.149, ...), kind=kLoop, calls=%fused_computation.354 | loop fusion | flops 23535616 | bytes 12609601 | tf_op jit(solution)/shard_map/convert_element_type | solution.py:154
  114.5 2.1 collective-permute-start.13
  116.7 1.9 reshape.2391
  120.5 2.7 multiply_reduce_fusion.2
  124.2 2.8 convert_reduce_fusion.2
  127.1 1.1 fusion.254
  128.6 1.7 fusion.219
  131.4 1.3 fusion.220
  135.2 2.0 collective-permute-start.14
  137.3 1.6 fusion.16
  138.8 1.7 fusion.18
  141.6 14.1 %all-reduce.2 = (f32[1,49,256]{2,0,1:T(1,128)S(1)}, f32[1,5,256]{2,0,1:T(1,128)S(1)}, f32[1,1024]{1,0:T(1,128)S(1)}) all-reduce(f32[1,49,256]{2,0,1:T(1,128)S(1)} %multiply_add_fusion.3, f32[1,5,256]{2,0,1:T(1,128)S(1)} %multiply_add_fusion.4, f32[1,1024]{1,0:T(1,128)S(1)} %bitcast.419), channel_id=1, replica_groups=mesh['section'=2,'lat'=4,'lon'=32] {'lat'}, use_global_device_ids=true, to_apply=%region_106.107 | all-reduce | flops 14848 | bytes 118784 | tf_op jit(solution)/shard_map/psum | solution.py:220
  155.7 141.7 %all-reduce = (f32[1,49,256]{2,0,1:T(1,128)S(1)}, f32[1,5,256]{2,0,1:T(1,128)S(1)}, f32[1,1024]{1,0:T(1,128)S(1)}) all-reduce(f32[1,49,256]{2,0,1:T(1,128)S(1)} %get-tuple-element.128, f32[1,5,256]{2,0,1:T(1,128)S(1)} %get-tuple-element.129, ...), channel_id=1, replica_groups=mesh['section'=2,'lat'=4,'lon'=32] {'lon'}, use_global_device_ids=true, to_apply=%region_107.108 | all-reduce | flops 14848 | bytes 118784 | tf_op jit(solution)/shard_map/psum | solution.py:220
  298.5 1.4 collective-permute-start.16
  299.9 1.3 collective-permute-start.17
  302.5 2.4 collective-permute-done.17
  305.2 4.9 %fusion.252 = bf16[1,2,4,68,256]{4,3,2,1,0:T(8,128)(2,1)S(1)} fusion(f32[2,4,68,256]{3,2,1,0:T(8,128)S(1)} %copy-done.9, f32[256]{0:T(256)S(1)} %bitcast.418, f32[4,68]{1,0:T(4,128)S(1)} %convert_element_type.1601, f32[256]{0:T(256)S(1)} %bitcast.223, bf16[2,7,74,256]{3,2,1,0:T(8,128)(2,1)S(1)} %get-tuple-element.145, f32[256]{0:T(256)S(1)} %bitcast.343, ...), kind=kLoop, calls=%fused_computation.427 | loop fusion | flops 24510464 | bytes 13446209 | tf_op jit(solution)/shard_map/broadcast_in_dim | solution.py:218
  311.0 136.9 %all-reduce.7.cloned.1.call-done = (f32[1,256,1024]{2,1,0:T(8,128)}, f32[1,1024,256]{2,1,0:T(8,128)}) async-done(((f32[1,256,1024]{2,1,0:T(8,128)}, f32[1,1024,256]{2,1,0:T(8,128)}), (f32[1,256,1024]{2,1,0:T(8,128)}, f32[1,1024,256]{2,1,0:T(8,128)})) %all-reduce.7.cloned.1.call-update) | async-done | bytes 2097168 | tf_op jit(solution)/shard_map/psum | solution.py:220
  447.8 2.4 broadcast_multiply_fusion.1
  450.3 1.1 broadcast_multiply_fusion
  (472 shorter events, 27.2 us)
Async XLA Ops:
  7.2 29.3 %copy-start = (bf16[1,256,1024]{2,1,0:T(8,128)(2,1)S(1)}, bf16[1,256,1024]{2,1,0:T(8,128)(2,1)}, u32[]{:S(2)}) copy-start(bf16[1,256,1024]{2,1,0:T(8,128)(2,1)} %param.13) | copy-start | bytes 1572868
  7.2 290.9 %all-reduce.9.cloned.1.call-start = ((), (), s32[]{:S(2)}) async-start(), calls=%async_computation.1 | async-start | bytes 4194304 | tf_op jit(solution)/shard_map/psum | solution.py:220
  7.2 19.4 %copy-start.131 = (bf16[1,5,256]{2,1,0:T(8,128)(2,1)S(1)}, bf16[1,5,256]{2,1,0:T(8,128)(2,1)}, u32[]{:S(2)}) copy-start(bf16[1,5,256]{2,1,0:T(8,128)(2,1)} %param.12) | copy-start | bytes 7684
  7.2 19.9 %copy-start.138 = (bf16[1,1024]{1,0:T(2,128)(2,1)S(1)}, bf16[1,1024]{1,0:T(2,128)(2,1)}, u32[]{:S(2)}) copy-start(bf16[1,1024]{1,0:T(2,128)(2,1)} %param.14) | copy-start | bytes 6148
  7.3 20.5 %copy-start.141 = (s32[4,68]{1,0:T(4,128)S(1)}, s32[4,68]{1,0:T(4,128)}, u32[]{:S(2)}) copy-start(s32[4,68]{1,0:T(4,128)} %param.10) | copy-start | bytes 3268
  7.3 20.5 %copy-start.37 = (bf16[1,49,256]{2,1,0:T(8,128)(2,1)S(1)}, bf16[1,49,256]{2,1,0:T(8,128)(2,1)}, u32[]{:S(2)}) copy-start(bf16[1,49,256]{2,1,0:T(8,128)(2,1)} %param.11) | copy-start | bytes 75268
  8.3 22.4 %copy-start.3 = (bf16[2,4,68,256]{3,2,1,0:T(8,128)(2,1)}, bf16[2,4,68,256]{3,2,1,0:T(8,128)(2,1)S(1)}, u32[]{:S(2)}) copy-start(bf16[2,4,68,256]{3,2,1,0:T(8,128)(2,1)S(1)} %copy_select_fusion) | copy-start | bytes 835588
  8.4 10.3 %collective-permute-start.1 = (bf16[2,4,3,256]{3,2,1,0:T(4,128)(2,1)S(1)}, bf16[2,4,3,256]{3,2,1,0:T(4,128)(2,1)S(1)}, u32[]{:S(2)}, u32[]{:S(2)}) collective-permute-start(bf16[2,4,3,256]{3,2,1,0:T(4,128)(2,1)S(1)} %get-tuple-element.169), channel_id=1, source_target_pairs={{1,0},{2,1},{3,2},{4,3},{5,4},{6,5},{7,6},{8,7},{9,8},{10,9},{11,1... | collective-permute-start | bytes 36872 | tf_op jit(solution)/shard_map/ppermute | solution.py:28
  16.8 7.1 %collective-permute-start = (bf16[2,4,3,256]{3,2,1,0:T(4,128)(2,1)S(1)}, bf16[2,4,3,256]{3,2,1,0:T(4,128)(2,1)S(1)}, u32[]{:S(2)}, u32[]{:S(2)}) collective-permute-start(bf16[2,4,3,256]{3,2,1,0:T(4,128)(2,1)S(1)} %get-tuple-element.168), channel_id=1, source_target_pairs={{0,1},{1,2},{2,3},{3,4},{4,5},{5,6},{6,7},{7,8},{8,9},{9,10},{10,1... | collective-permute-start | bytes 36872 | tf_op jit(solution)/shard_map/ppermute | solution.py:25
  18.7 50.7 %copy-start.38 = (f32[1,1,256]{2,1,0:T(1,128)}, f32[1,1,256]{2,1,0:T(1,128)S(1)}, u32[]{:S(2)}) copy-start(f32[1,1,256]{2,1,0:T(1,128)S(1)} %get-tuple-element.217) | copy-start | bytes 3076
  18.7 50.7 %copy-start.41 = (f32[1,1,256]{2,1,0:T(1,128)}, f32[1,1,256]{2,1,0:T(1,128)S(1)}, u32[]{:S(2)}) copy-start(f32[1,1,256]{2,1,0:T(1,128)S(1)} %get-tuple-element.218) | copy-start | bytes 3076
  24.0 4.0 collective-permute-start.2
  25.3 4.8 %collective-permute-start.3 = (bf16[2,3,74,256]{3,2,1,0:T(8,128)(2,1)S(1)}, bf16[2,3,74,256]{3,2,1,0:T(8,128)(2,1)S(1)}, u32[]{:S(2)}, u32[]{:S(2)}) collective-permute-start(bf16[2,3,74,256]{3,2,1,0:T(8,128)(2,1)S(1)} %get-tuple-element.159), channel_id=1, source_target_pairs={{32,0},{64,32},{96,64},{33,1},{65,33},{97,65},{34,2},{66,34},{98,6... | collective-permute-start | bytes 681992 | tf_op jit(solution)/shard_map/ppermute | solution.py:28
  27.2 8.4 %copy-start.128 = (f32[1,1,256]{2,1,0:T(1,128)}, f32[1,1,256]{2,1,0:T(1,128)S(1)}, u32[]{:S(2)}) copy-start(f32[1,1,256]{2,1,0:T(1,128)S(1)} %get-tuple-element.223) | copy-start | bytes 3076
  27.2 9.0 %copy-start.126 = (f32[1,1,256]{2,1,0:T(1,128)}, f32[1,1,256]{2,1,0:T(1,128)S(1)}, u32[]{:S(2)}) copy-start(f32[1,1,256]{2,1,0:T(1,128)S(1)} %get-tuple-element.225) | copy-start | bytes 3076
  27.8 7.8 %copy-start.47 = (f32[1,1,256]{2,1,0:T(1,128)}, f32[1,1,256]{2,1,0:T(1,128)S(1)}, u32[]{:S(2)}) copy-start(f32[1,1,256]{2,1,0:T(1,128)S(1)} %get-tuple-element.190) | copy-start | bytes 3076
  27.8 7.8 %copy-start.51 = (f32[1,1,256]{2,1,0:T(1,128)}, f32[1,1,256]{2,1,0:T(1,128)S(1)}, u32[]{:S(2)}) copy-start(f32[1,1,256]{2,1,0:T(1,128)S(1)} %get-tuple-element.191) | copy-start | bytes 3076
  27.8 7.8 %copy-start.55 = (f32[1,1,256]{2,1,0:T(1,128)}, f32[1,1,256]{2,1,0:T(1,128)S(1)}, u32[]{:S(2)}) copy-start(f32[1,1,256]{2,1,0:T(1,128)S(1)} %get-tuple-element.192) | copy-start | bytes 3076
  27.8 7.8 %copy-start.59 = (f32[1,1,256]{2,1,0:T(1,128)}, f32[1,1,256]{2,1,0:T(1,128)S(1)}, u32[]{:S(2)}) copy-start(f32[1,1,256]{2,1,0:T(1,128)S(1)} %get-tuple-element.193) | copy-start | bytes 3076
  27.8 7.8 %copy-start.63 = (f32[1,1,256]{2,1,0:T(1,128)}, f32[1,1,256]{2,1,0:T(1,128)S(1)}, u32[]{:S(2)}) copy-start(f32[1,1,256]{2,1,0:T(1,128)S(1)} %get-tuple-element.194) | copy-start | bytes 3076
  27.9 7.8 %copy-start.67 = (f32[1,1,256]{2,1,0:T(1,128)}, f32[1,1,256]{2,1,0:T(1,128)S(1)}, u32[]{:S(2)}) copy-start(f32[1,1,256]{2,1,0:T(1,128)S(1)} %get-tuple-element.195) | copy-start | bytes 3076
  27.9 7.8 %copy-start.71 = (f32[1,1,256]{2,1,0:T(1,128)}, f32[1,1,256]{2,1,0:T(1,128)S(1)}, u32[]{:S(2)}) copy-start(f32[1,1,256]{2,1,0:T(1,128)S(1)} %get-tuple-element.196) | copy-start | bytes 3076
  27.9 7.8 %copy-start.75 = (f32[1,1,256]{2,1,0:T(1,128)}, f32[1,1,256]{2,1,0:T(1,128)S(1)}, u32[]{:S(2)}) copy-start(f32[1,1,256]{2,1,0:T(1,128)S(1)} %get-tuple-element.197) | copy-start | bytes 3076
  27.9 7.8 %copy-start.79 = (f32[1,1,256]{2,1,0:T(1,128)}, f32[1,1,256]{2,1,0:T(1,128)S(1)}, u32[]{:S(2)}) copy-start(f32[1,1,256]{2,1,0:T(1,128)S(1)} %get-tuple-element.198) | copy-start | bytes 3076
  27.9 7.8 %copy-start.83 = (f32[1,1,256]{2,1,0:T(1,128)}, f32[1,1,256]{2,1,0:T(1,128)S(1)}, u32[]{:S(2)}) copy-start(f32[1,1,256]{2,1,0:T(1,128)S(1)} %get-tuple-element.199) | copy-start | bytes 3076
  27.9 7.8 %copy-start.87 = (f32[1,1,256]{2,1,0:T(1,128)}, f32[1,1,256]{2,1,0:T(1,128)S(1)}, u32[]{:S(2)}) copy-start(f32[1,1,256]{2,1,0:T(1,128)S(1)} %get-tuple-element.200) | copy-start | bytes 3076
  27.9 7.8 %copy-start.91 = (f32[1,1,256]{2,1,0:T(1,128)}, f32[1,1,256]{2,1,0:T(1,128)S(1)}, u32[]{:S(2)}) copy-start(f32[1,1,256]{2,1,0:T(1,128)S(1)} %get-tuple-element.201) | copy-start | bytes 3076
  27.9 7.8 %copy-start.95 = (f32[1,1,256]{2,1,0:T(1,128)}, f32[1,1,256]{2,1,0:T(1,128)S(1)}, u32[]{:S(2)}) copy-start(f32[1,1,256]{2,1,0:T(1,128)S(1)} %get-tuple-element.202) | copy-start | bytes 3076
  28.0 41.5 %copy-start.44 = (f32[1,1,256]{2,1,0:T(1,128)}, f32[1,1,256]{2,1,0:T(1,128)S(1)}, u32[]{:S(2)}) copy-start(f32[1,1,256]{2,1,0:T(1,128)S(1)} %get-tuple-element.189) | copy-start | bytes 3076
  41.1 10.1 %collective-permute-start.4 = (bf16[2,4,68,256]{3,2,1,0:T(8,128)(2,1)S(1)}, bf16[2,4,68,256]{3,2,1,0:T(8,128)(2,1)S(1)}, u32[]{:S(2)}, u32[]{:S(2)}) collective-permute-start(bf16[2,4,68,256]{3,2,1,0:T(8,128)(2,1)S(1)} %get-tuple-element.227), channel_id=1, source_target_pairs={{0,128},{1,129},{2,130},{3,131},{4,132},{5,133},{6,134},{7,135},{8... | collective-permute-start | bytes 835592 | tf_op jit(solution)/shard_map/ppermute | solution.py:36
  51.2 8.3 %copy-start.21 = (bf16[2,4,68,256]{3,2,1,0:T(8,128)(2,1)}, bf16[2,4,68,256]{3,2,1,0:T(8,128)(2,1)S(1)}, u32[]{:S(2)}) copy-start(bf16[2,4,68,256]{3,2,1,0:T(8,128)(2,1)S(1)} %collective-permute-done.4) | copy-start | bytes 835588
  51.2 23.4 %copy-start.5 = (bf16[2,4,68,256]{3,2,1,0:T(8,128)(2,1)}, bf16[2,4,68,256]{3,2,1,0:T(8,128)(2,1)S(1)}, u32[]{:S(2)}) copy-start(bf16[2,4,68,256]{3,2,1,0:T(8,128)(2,1)S(1)} %broadcast_select_fusion.5) | copy-start | bytes 835588
  51.3 3.8 collective-permute-start.6
  51.6 7.1 %collective-permute-start.5 = (bf16[2,4,3,256]{3,2,1,0:T(4,128)(2,1)S(1)}, bf16[2,4,3,256]{3,2,1,0:T(4,128)(2,1)S(1)}, u32[]{:S(2)}, u32[]{:S(2)}) collective-permute-start(bf16[2,4,3,256]{3,2,1,0:T(4,128)(2,1)S(1)} %get-tuple-element.166), channel_id=1, source_target_pairs={{0,1},{1,2},{2,3},{3,4},{4,5},{5,6},{6,7},{7,8},{8,9},{9,10},{10,1... | collective-permute-start | bytes 36872 | tf_op jit(solution)/shard_map/ppermute | solution.py:25
  59.5 6.5 %collective-permute-start.7 = (bf16[2,3,74,256]{3,2,1,0:T(8,128)(2,1)}, bf16[2,3,74,256]{3,2,1,0:T(8,128)(2,1)S(1)}, u32[]{:S(2)}, u32[]{:S(2)}) collective-permute-start(bf16[2,3,74,256]{3,2,1,0:T(8,128)(2,1)} %get-tuple-element.154), channel_id=1, source_target_pairs={{0,32},{32,64},{64,96},{1,33},{33,65},{65,97},{2,34},{34,66},{66,9... | collective-permute-start | bytes 681992 | tf_op jit(solution)/shard_map/ppermute | solution.py:25
  63.5 5.2 %collective-permute-start.8 = (bf16[2,3,74,256]{3,2,1,0:T(8,128)(2,1)S(1)}, bf16[2,3,74,256]{3,2,1,0:T(8,128)(2,1)S(1)}, u32[]{:S(2)}, u32[]{:S(2)}) collective-permute-start(bf16[2,3,74,256]{3,2,1,0:T(8,128)(2,1)S(1)} %get-tuple-element.155), channel_id=1, source_target_pairs={{32,0},{64,32},{96,64},{33,1},{65,33},{97,65},{34,2},{66,34},{98,6... | collective-permute-start | bytes 681992 | tf_op jit(solution)/shard_map/ppermute | solution.py:28
  92.3 14.1 %copy-start.30 = (bf16[544,1024]{1,0:T(8,128)(2,1)S(1)}, bf16[544,1024]{1,0:T(8,128)(2,1)}, u32[]{:S(2)}) copy-start(bf16[544,1024]{1,0:T(8,128)(2,1)} %get-tuple-element.143) | copy-start | bytes 3342340
  92.3 14.1 %copy-start.125 = (f32[1,1,256]{2,1,0:T(1,128)S(1)}, f32[1,1,256]{2,1,0:T(1,128)}, u32[]{:S(2)}) copy-start(f32[1,1,256]{2,1,0:T(1,128)} %get-tuple-element.224) | copy-start | bytes 3076
  92.3 3.7 collective-permute-start.10
  92.3 7.1 %collective-permute-start.9 = (bf16[2,4,3,256]{3,2,1,0:T(4,128)(2,1)S(1)}, bf16[2,4,3,256]{3,2,1,0:T(4,128)(2,1)S(1)}, u32[]{:S(2)}, u32[]{:S(2)}) collective-permute-start(bf16[2,4,3,256]{3,2,1,0:T(4,128)(2,1)S(1)} %get-tuple-element.164), channel_id=1, source_target_pairs={{0,1},{1,2},{2,3},{3,4},{4,5},{5,6},{6,7},{7,8},{8,9},{9,10},{10,1... | collective-permute-start | bytes 36872 | tf_op jit(solution)/shard_map/ppermute | solution.py:25
  99.5 8.4 %collective-permute-start.11 = (bf16[2,3,74,256]{3,2,1,0:T(8,128)(2,1)S(1)}, bf16[2,3,74,256]{3,2,1,0:T(8,128)(2,1)S(1)}, u32[]{:S(2)}, u32[]{:S(2)}) collective-permute-start(bf16[2,3,74,256]{3,2,1,0:T(8,128)(2,1)S(1)} %get-tuple-element.150), channel_id=1, source_target_pairs={{0,32},{32,64},{64,96},{1,33},{33,65},{65,97},{2,34},{34,66},{66,9... | collective-permute-start | bytes 681992 | tf_op jit(solution)/shard_map/ppermute | solution.py:25
  104.9 3.9 collective-permute-start.12
  114.5 6.0 %collective-permute-start.13 = (bf16[2,4,68,256]{3,2,1,0:T(8,128)(2,1)}, bf16[2,4,68,256]{3,2,1,0:T(8,128)(2,1)}, u32[]{:S(2)}, u32[]{:S(2)}) collective-permute-start(bf16[2,4,68,256]{3,2,1,0:T(8,128)(2,1)} %add_convert_fusion.1), channel_id=1, source_target_pairs={{128,0},{129,1},{130,2},{131,3},{132,4},{133,5},{134,6},{135,7},{1... | collective-permute-start | bytes 835592 | tf_op jit(solution)/shard_map/ppermute | solution.py:36
  135.1 162.9 %collective-permute-start.15 = (bf16[2,4,3,256]{3,2,1,0:T(4,128)(2,1)S(1)}, bf16[2,4,3,256]{3,2,1,0:T(4,128)(2,1)S(1)}, u32[]{:S(2)}, u32[]{:S(2)}) collective-permute-start(bf16[2,4,3,256]{3,2,1,0:T(4,128)(2,1)S(1)} %get-tuple-element.163), channel_id=1, source_target_pairs={{1,0},{2,1},{3,2},{4,3},{5,4},{6,5},{7,6},{8,7},{9,8},{10,9},{11,1... | collective-permute-start | bytes 36872 | tf_op jit(solution)/shard_map/ppermute | solution.py:28
  135.2 162.8 %collective-permute-start.14 = (bf16[2,4,3,256]{3,2,1,0:T(4,128)(2,1)S(1)}, bf16[2,4,3,256]{3,2,1,0:T(4,128)(2,1)S(1)}, u32[]{:S(2)}, u32[]{:S(2)}) collective-permute-start(bf16[2,4,3,256]{3,2,1,0:T(4,128)(2,1)S(1)} %get-tuple-element.162), channel_id=1, source_target_pairs={{0,1},{1,2},{2,3},{3,4},{4,5},{5,6},{6,7},{7,8},{8,9},{9,10},{10,1... | collective-permute-start | bytes 36872 | tf_op jit(solution)/shard_map/ppermute | solution.py:25
  141.1 306.7 %all-reduce.7.cloned.1.call-start = ((), (), s32[]{:S(2)}) async-start(), calls=%async_computation | async-start | bytes 4194304 | tf_op jit(solution)/shard_map/psum | solution.py:220
  298.5 4.0 collective-permute-start.16
  299.9 4.9 %collective-permute-start.17 = (bf16[2,3,74,256]{3,2,1,0:T(8,128)(2,1)S(1)}, bf16[2,3,74,256]{3,2,1,0:T(8,128)(2,1)S(1)}, u32[]{:S(2)}, u32[]{:S(2)}) collective-permute-start(bf16[2,3,74,256]{3,2,1,0:T(8,128)(2,1)S(1)} %get-tuple-element.147), channel_id=1, source_target_pairs={{32,0},{64,32},{96,64},{33,1},{65,33},{97,65},{34,2},{66,34},{98,6... | collective-permute-start | bytes 681992 | tf_op jit(solution)/shard_map/ppermute | solution.py:28
  (116 other events, 409.4 us)
Sparse Core Ops, SparseCore 0:
  141.2 63.1 all-reduce.8
  298.2 149.6 all-reduce.6
